TPU v7x, 512 devices: a whole 4x8x8 slice. The times are simulated.
512 devices in a mesh: dp: 8 (over y), expert: 64 (over z, x, core).
Axes of the slice: x: 4, y: 8, z: 8, core: 2. Of those that a mesh axis runs over, the one named last changes fastest.
Arguments:
- tokens: bfloat16 [4096, 4096], P('expert', 'dp'), may hold values from -6 to 6
- expert_ids: int32 [4096, 8], P('expert'), may hold values from 0 to 63, all different within a row; in each aligned block of 64 rows (0 to 63, 64 to 127, ...) at most 16 rows name the same one
- gate_weights: float32 [4096, 8], P('expert'), may hold values from 0.05 to 1
- gate_proj: bfloat16 [64, 4096, 1536], P('expert', 'dp'), may hold values from -0.09375 to 0.09375
- up_proj: bfloat16 [64, 4096, 1536], P('expert', 'dp'), may hold values from -0.09375 to 0.09375
- down_proj: bfloat16 [64, 1536, 4096], P('expert', None, 'dp'), may hold values from -0.15625 to 0.15625
Outputs:
- combined: bfloat16 [4096, 4096], P('expert', 'dp')
Inputs may be any that keep to these rules, and one draw needn't show every extreme that they name: `expert_ids`: each row names 8 different experts. Among the 64 rows of one device (one aligned block), no expert is named by more than 16 rows, and in every draw some expert is named by exactly 16 rows of some block.
All inputs are finite; a program needn't handle non-finite values.
Results may differ from a plain program's by a relative error of at most 0.029.
Values may be sent and summed in bfloat16 or wider, within the bound.
A program may use at most 64 MiB of HBM per device.

v0:
```python
import jax
import jax.numpy as jnp
from jax import lax
from jax.sharding import PartitionSpec as P


def block_places(block_ids, expert_count, capacity):
    tok_count, top_count = block_ids.shape
    flat_ids = block_ids.reshape(tok_count * top_count)
    matches = (flat_ids[:, None] == jnp.arange(expert_count, dtype=jnp.int32)[None, :]).astype(
        jnp.int32
    )
    earlier = jnp.cumsum(matches, axis=0) - matches
    slot_index = jnp.sum(earlier * matches, axis=1)
    return (flat_ids * capacity + slot_index).reshape(tok_count, top_count)


def body(tokens, expert_ids, gate_weights, gate_proj, up_proj, down_proj):
    tok_count, top_count = expert_ids.shape
    row_width = tokens.shape[1]
    sources = lax.axis_size("expert")
    capacity = 2 * tok_count * top_count // sources
    positions = jnp.arange(sources * capacity, dtype=jnp.int32)
    places = block_places(expert_ids, sources, capacity)
    matches = places[:, :, None] == positions[None, None, :]
    weighting = jnp.sum(jnp.where(matches, gate_weights[:, :, None], 0.0), axis=1)
    chosen = jnp.any(matches, axis=1).astype(jnp.bfloat16)
    outgoing = lax.dot_general(
        chosen, tokens, (((0,), (0,)), ((), ())), preferred_element_type=jnp.float32
    ).astype(jnp.bfloat16)
    incoming = lax.all_to_all(
        outgoing.reshape(sources, capacity, row_width),
        "expert",
        split_axis=0,
        concat_axis=0,
        tiled=True,
    )
    expert_rows = incoming.reshape(sources * capacity, row_width)
    gate_part = jnp.dot(expert_rows, gate_proj[0], preferred_element_type=jnp.float32)
    up_part = jnp.dot(expert_rows, up_proj[0], preferred_element_type=jnp.float32)
    gate_sum, up_sum = (
        lax.psum(gate_part.astype(jnp.bfloat16), "dp").astype(jnp.float32),
        lax.psum(up_part.astype(jnp.bfloat16), "dp").astype(jnp.float32),
    )
    hidden = (jax.nn.silu(gate_sum) * up_sum).astype(jnp.bfloat16)
    expert_out = jnp.dot(hidden, down_proj[0], preferred_element_type=jnp.float32).astype(
        jnp.bfloat16
    )
    returned = lax.all_to_all(
        expert_out.reshape(sources, capacity, row_width),
        "expert",
        split_axis=0,
        concat_axis=0,
        tiled=True,
    )
    returned_flat = returned.reshape(sources * capacity, row_width)
    weight_high = weighting.astype(jnp.bfloat16)
    weight_low = (weighting - weight_high.astype(jnp.float32)).astype(jnp.bfloat16)
    combined = jnp.dot(weight_high, returned_flat, preferred_element_type=jnp.float32)
    combined = combined + jnp.dot(weight_low, returned_flat, preferred_element_type=jnp.float32)
    return combined.astype(jnp.bfloat16)


def solution(mesh):
    placed = (
        P("expert", "dp"),
        P("expert", None),
        P("expert", None),
        P("expert", "dp", None),
        P("expert", "dp", None),
        P("expert", None, "dp"),
    )
    return jax.shard_map(
        body, mesh=mesh, in_specs=placed, out_specs=P("expert", "dp"), check_vma=False
    )
```

profile of v0, /device:TPU:1, one launch (start us, length us, event | category | flops | bytes accessed | tf_op | source)
XLA Modules:
  0.0 266.4 jit_solution(7959144195242189206)
XLA Ops:
  6.5 0.0 copy-start
  6.5 0.0 all-reduce.3.cloned.1.call-start
  6.5 0.9 copy.21
  7.4 0.1 eq.42
  7.5 0.1 eq.38
  7.6 1.2 reduce-window.6
  8.8 0.2 slice_reduce_fusion
  9.1 0.1 fusion.19
  9.2 0.1 reduce_sum.21
  9.3 0.1 copy.24
  9.4 0.7 multiply_add_fusion
  10.1 0.1 copy.25
  10.2 0.7 fusion.7
  10.9 1.3 convolution_convert_fusion.2
  12.2 42.6 %all_to_all.10 = bf16[64,16,512]{2,1,0:T(8,128)(2,1)S(1)} all-to-all(bf16[64,16,512]{2,1,0:T(8,128)(2,1)S(1)} %bitcast.42), channel_id=1, replica_groups=mesh['dp'=8,'expert'=64] {'expert'}, dimensions={0} | all-to-all | bytes 2097152 | tf_op jit(solution)/shard_map/all_to_all | solution.py:31
  54.8 0.0 copy-done
  54.8 0.0 copy-start.2
  54.8 3.5 %convolution_convert_fusion = bf16[1024,1536]{1,0:T(8,128)(2,1)} fusion(bf16[1024,512]{1,0:T(8,128)(2,1)S(1)} %bitcast.44, bf16[1,512,1536]{2,1,0:T(8,128)(2,1)S(1)} %copy-done), kind=kOutput, calls=%fused_computation.7 | convolution fusion | flops 1612185600 | bytes 5767168 | tf_op jit(solution)/shard_map/dot_general | solution.py:40
  58.3 0.0 copy-done.2
  58.3 3.4 %convolution_convert_fusion.1 = bf16[1024,1536]{1,0:T(8,128)(2,1)} fusion(bf16[1024,512]{1,0:T(8,128)(2,1)S(1)} %bitcast.45, bf16[1,512,1536]{2,1,0:T(8,128)(2,1)S(1)} %copy-done.2), kind=kOutput, calls=%fused_computation.8 | convolution fusion | flops 1612185600 | bytes 5767168 | tf_op jit(solution)/shard_map/dot_general | solution.py:39
  61.8 0.0 all-reduce.3.cloned.1.call-update
  61.8 151.3 %all-reduce.3.cloned.1.call-done = (bf16[1024,1536]{1,0:T(8,128)(2,1)}, bf16[1024,1536]{1,0:T(8,128)(2,1)}) async-done(((bf16[1024,1536]{1,0:T(8,128)(2,1)}, bf16[1024,1536]{1,0:T(8,128)(2,1)}), (bf16[1024,1536]{1,0:T(8,128)(2,1)}, bf16[1024,1536]{1,0:T(8,128)(2,1)})) %all-reduce.3.cloned.1.call-update) | async-done | bytes 6291472 | tf_op jit(solution)/shard_map/psum | solution.py:43
  213.1 0.0 copy-start.1
  213.1 6.2 %fusion.11 = bf16[1024,512]{1,0:T(8,128)(2,1)} fusion(bf16[1,1536,512]{2,1,0:T(8,128)(2,1)} %param.11, bf16[1024,1536]{1,0:T(8,128)(2,1)} %get-tuple-element.5, bf16[1024,1536]{1,0:T(8,128)(2,1)} %get-tuple-element.6), kind=kOutput, calls=%fused_computation.16 | convolution fusion | flops 1623719936 | bytes 8912896 | tf_op jit(solution)/shard_map/dot_general | solution.py:46
  219.3 11.0 %all-to-all-start.1 = ((bf16[64,16,512]{2,1,0:T(8,128)(2,1)}), bf16[64,16,512]{2,1,0:T(8,128)(2,1)S(1)}, u32[]{:S(2)}, u32[]{:S(2)}) async-start(bf16[64,16,512]{2,1,0:T(8,128)(2,1)} %bitcast.43), calls=%async_computation.1 | async-start | bytes 2097152 | tf_op jit(solution)/shard_map/all_to_all | solution.py:49
  230.4 0.0 copy-done.1
  230.4 0.1 copy.26
  230.5 0.7 select_reduce_fusion
  231.2 27.2 %all-to-all-done.1 = bf16[64,16,512]{2,1,0:T(8,128)(2,1)S(1)} async-done(((bf16[64,16,512]{2,1,0:T(8,128)(2,1)}), bf16[64,16,512]{2,1,0:T(8,128)(2,1)S(1)}, u32[]{:S(2)}, u32[]{:S(2)}) %all-to-all-start.1) | async-done | bytes 1048608 | tf_op jit(solution)/shard_map/all_to_all | solution.py:49
  258.3 0.3 fusion.22
  258.6 0.9 fusion.16
  (3 shorter events, 0.1 us)
Async XLA Ops:
  6.5 48.3 %copy-start = (bf16[1,512,1536]{2,1,0:T(8,128)(2,1)S(1)}, bf16[1,512,1536]{2,1,0:T(8,128)(2,1)}, u32[]{:S(2)}) copy-start(bf16[1,512,1536]{2,1,0:T(8,128)(2,1)} %param.10) | copy-start | bytes 4718596
  6.5 206.6 %all-reduce.3.cloned.1.call-start = ((), (), s32[]{:S(2)}) async-start(), calls=%async_computation.2 | async-start | bytes 12582912 | tf_op jit(solution)/shard_map/psum | solution.py:43
  54.8 3.5 %copy-start.2 = (bf16[1,512,1536]{2,1,0:T(8,128)(2,1)S(1)}, bf16[1,512,1536]{2,1,0:T(8,128)(2,1)}, u32[]{:S(2)}) copy-start(bf16[1,512,1536]{2,1,0:T(8,128)(2,1)} %param.9) | copy-start | bytes 4718596
  213.1 17.3 %copy-start.1 = (f32[64,8]{0,1:T(8,128)S(1)}, f32[64,8]{0,1:T(8,128)}, u32[]{:S(2)}) copy-start(f32[64,8]{0,1:T(8,128)} %param.8) | copy-start | bytes 6148
  219.3 39.0 %all-to-all-start.1 = ((bf16[64,16,512]{2,1,0:T(8,128)(2,1)}), bf16[64,16,512]{2,1,0:T(8,128)(2,1)S(1)}, u32[]{:S(2)}, u32[]{:S(2)}) async-start(bf16[64,16,512]{2,1,0:T(8,128)(2,1)} %bitcast.43), calls=%async_computation.1 | async-start | bytes 2097152 | tf_op jit(solution)/shard_map/all_to_all | solution.py:49
Sparse Core Ops, SparseCore 0:
  61.9 151.1 all-reduce.2
where the time goes:
time: 267 us; the launch traced here: 266 us
  waiting for transfers between devices  178 us (67%)
  blocking collectives  42.6 us (16%)
  matrix products  15.7 us (6%)
  between operations  13.5 us (5%)
  starting transfers between devices  11 us (4%)
  other arithmetic  3.49 us (1%)
    psum x1, waiting for transfers between devices, body(): lax.psum(up_part.astype(jnp.bfloat16), 'dp').astype(jnp.float32)  151 us
    all_to_all x1, blocking collectives, body(): lax.all_to_all(outgoing.reshape(sources, capacity, row_width), 'expert',...  42.6 us
    all_to_all x1, waiting for transfers between devices, body(): lax.all_to_all(expert_out.reshape(sources, capacity, row_width), 'expert'...  27.2 us
    all_to_all x1, starting transfers between devices, body(): lax.all_to_all(expert_out.reshape(sources, capacity, row_width), 'expert'...  11 us
    dot_general x1, matrix products, body(): jnp.dot(hidden, down_proj[0], preferred_element_type=jnp.float32)  6.23 us
  transfers between devices with their start and end apart: 2, of which 2 were waited for; matrix products, arithmetic and copies ran while one was open for 0% of the time, Pallas kernels for 0%

commit v1 on v0

--- a/solution.py
+++ b/solution.py
@@ -40,7 +40,7 @@
     up_part = jnp.dot(expert_rows, up_proj[0], preferred_element_type=jnp.float32)
     gate_sum, up_sum = (
         lax.psum(gate_part.astype(jnp.bfloat16), "dp").astype(jnp.float32),
-        lax.psum(up_part.astype(jnp.bfloat16), "dp").astype(jnp.float32),
+        jnp.sum(lax.all_gather(up_part.astype(jnp.bfloat16), "dp"), axis=0).astype(jnp.float32),
     )
     hidden = (jax.nn.silu(gate_sum) * up_sum).astype(jnp.bfloat16)
     expert_out = jnp.dot(hidden, down_proj[0], preferred_element_type=jnp.float32).astype(

time: 267 us -> 461 us (1.73)
  waiting for transfers between devices: 178 us -> 355 us
  other arithmetic: 3.49 us -> 19 us
    all_gather x0 -> x1, waiting for transfers between devices: none -> 246 us  [body(): lax.all_gather(up_part.astype(jnp.bfloat16), 'dp')]
    psum x1, waiting for transfers between devices: 151 us -> 81.7 us  [body(): lax.psum(gate_part.astype(jnp.bfloat16), 'dp').astype(jnp.float32)]
    reduce_sum x0 -> x1, other arithmetic: none -> 15.6 us  [body(): jnp.sum(lax.all_gather(up_part.astype(jnp.bfloat16), 'dp'), axis=0)]
  transfers between devices with their start and end apart: 2 -> 3, of which waited for: 2 -> 3; matrix products, arithmetic and copies ran while one was open for 0% -> 5% of each run, Pallas kernels for 0% -> 0%
where the time goes in v1:
time: 461 us
  waiting for transfers between devices  355 us (77%)
  blocking collectives  42.6 us (9%)
  other arithmetic  19 us (4%)
  matrix products  17.1 us (4%)
  between operations  13.5 us (3%)
  starting transfers between devices  11.9 us (3%)
    all_gather x1, waiting for transfers between devices, body(): lax.all_gather(up_part.astype(jnp.bfloat16), 'dp')  246 us
    psum x1, waiting for transfers between devices, body(): lax.psum(gate_part.astype(jnp.bfloat16), 'dp').astype(jnp.float32)  81.7 us
    all_to_all x1, blocking collectives, body(): lax.all_to_all(outgoing.reshape(sources, capacity, row_width), 'expert',...  42.6 us
    all_to_all x1, waiting for transfers between devices, body(): lax.all_to_all(expert_out.reshape(sources, capacity, row_width), 'expert'...  27.2 us
    reduce_sum x1, other arithmetic, body(): jnp.sum(lax.all_gather(up_part.astype(jnp.bfloat16), 'dp'), axis=0)  15.6 us
    all_to_all x1, starting transfers between devices, body(): lax.all_to_all(expert_out.reshape(sources, capacity, row_width), 'expert'...  11.9 us
  transfers between devices with their start and end apart: 3, of which 3 were waited for; matrix products, arithmetic and copies ran while one was open for 5% of the time, Pallas kernels for 0%

profile of v1, /device:TPU:1, one launch (start us, length us, event | category | flops | bytes accessed | tf_op | source)
XLA Modules:
  0.0 460.8 jit_solution(11014268018112297982)
XLA Ops:
  6.5 0.0 copy-start
  6.5 0.0 all-gather.3.cloned.1.call-start
  6.5 0.9 copy.21
  7.4 0.1 eq.42
  7.5 0.1 eq.38
  7.6 1.2 reduce-window.6
  8.8 0.2 slice_reduce_fusion
  9.1 0.1 fusion.19
  9.2 0.1 reduce_sum.33
  9.3 0.1 copy.24
  9.4 0.7 multiply_add_fusion
  10.1 0.1 copy.25
  10.2 0.7 fusion.7
  10.9 1.3 convolution_convert_fusion.2
  12.2 42.6 %all_to_all.10 = bf16[64,16,512]{2,1,0:T(8,128)(2,1)S(1)} all-to-all(bf16[64,16,512]{2,1,0:T(8,128)(2,1)S(1)} %bitcast.44), channel_id=1, replica_groups=mesh['dp'=8,'expert'=64] {'expert'}, dimensions={0} | all-to-all | bytes 2097152 | tf_op jit(solution)/shard_map/all_to_all | solution.py:31
  54.8 0.0 copy-done
  54.8 3.5 convolution_convert_fusion
  58.4 0.0 all-gather.3.cloned.1.call-update
  58.4 0.0 all-reduce.2.cloned.1.call-start
  58.5 4.8 %convolution_convert_fusion.1 = bf16[1024,1536]{1,0:T(8,128)(2,1)} fusion(bf16[1024,512]{1,0:T(8,128)(2,1)S(1)} %bitcast.46, bf16[1,512,1536]{2,1,0:T(8,128)(2,1)} %param.9), kind=kOutput, calls=%fused_computation.8 | convolution fusion | flops 1612185600 | bytes 5767168 | tf_op jit(solution)/shard_map/dot_general | solution.py:39
  63.3 0.0 all-reduce.2.cloned.1.call-update
  63.3 246.1 %all-gather.3.cloned.1.call-done = bf16[8192,1536]{1,0:T(8,128)(2,1)} async-done(((bf16[1024,1536]{1,0:T(8,128)(2,1)}), bf16[8192,1536]{1,0:T(8,128)(2,1)}) %all-gather.3.cloned.1.call-update) | async-done | bytes 25165840 | tf_op jit(solution)/shard_map/all_gather | solution.py:43
  309.4 15.6 %reduce_sum.35 = bf16[1024,1536]{1,0:T(8,128)(2,1)} reduce(bf16[8,1024,1536]{2,1,0:T(8,128)(2,1)} %bitcast.41, bf16[]{:T(256)} %constant.16.clone.1), dimensions={0}, to_apply=%region_6.7 | reduce | flops 11010048 | bytes 28311554 | tf_op jit(solution)/shard_map/reduce_sum | solution.py:43
  324.9 0.0 copy-start.1
  324.9 81.7 %all-reduce.2.cloned.1.call-done = bf16[1024,1536]{1,0:T(8,128)(2,1)} async-done(((bf16[1024,1536]{1,0:T(8,128)(2,1)}), bf16[1024,1536]{1,0:T(8,128)(2,1)}) %all-reduce.2.cloned.1.call-update) | async-done | bytes 3145744 | tf_op jit(solution)/shard_map/psum | solution.py:42
  406.7 6.2 %fusion.11 = bf16[1024,512]{1,0:T(8,128)(2,1)} fusion(bf16[1,1536,512]{2,1,0:T(8,128)(2,1)} %param.11, bf16[1024,1536]{1,0:T(8,128)(2,1)} %reduce_sum.35, bf16[1024,1536]{1,0:T(8,128)(2,1)} %all-reduce.2.cloned.1.call-done), kind=kOutput, calls=%fused_computation.16 | convolution fusion | flops 1623719936 | bytes 8912896 | tf_op jit(solution)/shard_map/dot_general | solution.py:46
  412.9 11.9 %all-to-all-start.1 = ((bf16[64,16,512]{2,1,0:T(8,128)(2,1)}), bf16[64,16,512]{2,1,0:T(8,128)(2,1)S(1)}, u32[]{:S(2)}, u32[]{:S(2)}) async-start(bf16[64,16,512]{2,1,0:T(8,128)(2,1)} %bitcast.47), calls=%async_computation.1 | async-start | bytes 2097152 | tf_op jit(solution)/shard_map/all_to_all | solution.py:49
  424.7 0.0 copy-done.1
  424.8 0.1 copy.26
  424.8 0.7 select_reduce_fusion
  425.6 27.2 %all-to-all-done.1 = bf16[64,16,512]{2,1,0:T(8,128)(2,1)S(1)} async-done(((bf16[64,16,512]{2,1,0:T(8,128)(2,1)}), bf16[64,16,512]{2,1,0:T(8,128)(2,1)S(1)}, u32[]{:S(2)}, u32[]{:S(2)}) %all-to-all-start.1) | async-done | bytes 1048608 | tf_op jit(solution)/shard_map/all_to_all | solution.py:49
  452.7 0.3 fusion.22
  453.0 0.9 fusion.16
  (3 shorter events, 0.1 us)
Async XLA Ops:
  6.5 48.3 %copy-start = (bf16[1,512,1536]{2,1,0:T(8,128)(2,1)S(1)}, bf16[1,512,1536]{2,1,0:T(8,128)(2,1)}, u32[]{:S(2)}) copy-start(bf16[1,512,1536]{2,1,0:T(8,128)(2,1)} %param.10) | copy-start | bytes 4718596
  6.5 302.9 %all-gather.3.cloned.1.call-start = ((), (), s32[]{:S(2)}) async-start(), calls=%async_computation.3 | async-start | bytes 28311552 | tf_op jit(solution)/shard_map/all_gather | solution.py:43
  58.4 348.3 %all-reduce.2.cloned.1.call-start = ((), (), s32[]{:S(2)}) async-start(), calls=%async_computation.2 | async-start | bytes 6291456 | tf_op jit(solution)/shard_map/psum | solution.py:42
  324.9 99.8 %copy-start.1 = (f32[64,8]{0,1:T(8,128)S(1)}, f32[64,8]{0,1:T(8,128)}, u32[]{:S(2)}) copy-start(f32[64,8]{0,1:T(8,128)} %param.8) | copy-start | bytes 6148
  412.9 39.9 %all-to-all-start.1 = ((bf16[64,16,512]{2,1,0:T(8,128)(2,1)}), bf16[64,16,512]{2,1,0:T(8,128)(2,1)S(1)}, u32[]{:S(2)}, u32[]{:S(2)}) async-start(bf16[64,16,512]{2,1,0:T(8,128)(2,1)} %bitcast.47), calls=%async_computation.1 | async-start | bytes 2097152 | tf_op jit(solution)/shard_map/all_to_all | solution.py:49
Sparse Core Ops, SparseCore 0:
  58.5 250.8 all-gather.2
  311.8 94.8 all-reduce.1
